TPU v7x, 256 devices: a whole 4x4x8 slice. The times are simulated.
256 devices in a mesh: tok: 16 (over y, x), feat: 16 (over z, core).
Axes of the slice: x: 4, y: 4, z: 8, core: 2. Of those that a mesh axis runs over, the one named last changes fastest.
Arguments:
- calib: float32 [16384, 22016], P('tok', 'feat')
- teacher_w: bfloat16 [22016, 256], P('feat'), may hold values from -6 to 6
- mask: int32 [172, 2], replicated, may hold values from 0 to 1, as said below
Outputs:
- solution: float32 [22016, 256], P('feat')
- residual: float32 [22016, 256], P('feat')
Inputs may be any that keep to these rules, and one draw needn't show every extreme that they name: `mask`: every column block has at least one row block with 1.
All inputs are finite; a program needn't handle non-finite values.
Results may differ from a plain program's by a relative error of at most 0.0003.
Values sent between devices are 32-bit elements; how exact they have to be, the bound alone decides.
No kernel may reach another device: no remote copies, remote signals or barrier semaphores. Data moves between devices by JAX's collectives and lax.ppermute only.
A program may use at most 64 MiB of HBM per device.

v0:
```python
import jax
import jax.numpy as jnp
from jax import lax
from jax.sharding import PartitionSpec as P

BLOCK = 128
ITERS = 2
DAMP_REL = 0.2


def matmul(left, right):
    return jnp.dot(left, right, precision=lax.Precision.HIGHEST, preferred_element_type=jnp.float32)


def back_product(left, right):
    return lax.dot_general(
        left,
        right,
        (((0,), (0,)), ((), ())),
        precision=lax.Precision.HIGHEST,
        preferred_element_type=jnp.float32,
    )


def col_norm(values):
    return lax.psum(jnp.sum(values * values, axis=0), "feat")


def on_device(calib, teacher_w, mask):
    feat_count = lax.axis_size("feat")
    feat_place = lax.axis_index("feat")
    rows_dev = calib.shape[0]
    din_dev = calib.shape[1]
    share = rows_dev // feat_count
    first_row = feat_place * din_dev
    block_ids = (first_row + jnp.arange(din_dev, dtype=jnp.int32)) // BLOCK
    onehot = (block_ids[:, None] == jnp.arange(mask.shape[0], dtype=jnp.int32)[None, :]).astype(
        jnp.float32
    )
    live_blocks = matmul(onehot, mask.astype(jnp.float32))
    live = jnp.repeat(live_blocks, BLOCK, axis=1)
    total = lax.psum(jnp.sum(calib * calib), ("tok", "feat"))
    damp = DAMP_REL * total / (din_dev * feat_count)

    def gram(vec):
        rows_out = lax.psum(matmul(calib, vec), "feat")
        partial_back = back_product(calib, rows_out)
        own_rows = lax.dynamic_slice_in_dim(rows_out, feat_place * share, share, 0)
        summed = lax.psum(partial_back, "tok")
        return (live * summed, own_rows)

    targets, unused_rows = gram(teacher_w.astype(jnp.float32))
    solution = jnp.zeros_like(targets)
    residual = targets
    direction = targets
    norm_now = col_norm(residual)
    for step in range(ITERS):
        image_raw, own_rows = gram(direction)
        image = image_raw + damp * direction
        curvature = lax.psum(jnp.sum(direction * image, axis=0), "feat")
        alpha = norm_now / curvature
        solution = solution + alpha * direction
        residual = residual - alpha * image
        fresh = col_norm(residual)
        direction = residual + fresh / norm_now * direction
        norm_now = fresh
    return (solution, residual)


def solution(mesh):
    in_specs = (P("tok", "feat"), P("feat", None), P())
    out_specs = (P("feat", None), P("feat", None))
    return jax.shard_map(
        on_device, mesh=mesh, in_specs=in_specs, out_specs=out_specs, check_vma=False
    )
```

profile of v0, /device:TPU:1, one launch (start us, length us, event | category | flops | bytes accessed | tf_op | source)
XLA Modules:
  0.0 783.0 jit_solution(17692124888101686545)
XLA Ops:
  7.2 0.0 copy-start
  7.2 0.0 all-reduce.8.cloned.1.call-start
  7.2 1.0 copy-done
  8.3 8.2 %fusion.8 = f32[1024,256]{1,0:T(8,128)} fusion(f32[1024,1376]{0,1:T(8,128)} %param.3, bf16[1376,256]{1,0:T(8,128)(2,1)S(1)} %copy-done), kind=kOutput, calls=%fused_computation.32 | convolution fusion | flops 4328521728 | bytes 7389184 | tf_op jit(solution)/shard_map/dot_general | solution.py:12
  16.5 0.0 all-reduce.8.cloned.1.call-update
  16.5 0.0 all-reduce.10.cloned.1.call-start
  16.6 115.3 %all-reduce.8.cloned.1.call-done = f32[1024,256]{1,0:T(8,128)} async-done(((f32[1024,256]{1,0:T(8,128)}), f32[1024,256]{1,0:T(8,128)}) %all-reduce.8.cloned.1.call-update) | async-done | bytes 1048592 | tf_op jit(solution)/shard_map/psum | solution.py:46
  131.8 8.7 %convolution_bitcast_fusion.2 = f32[1376,256]{1,0:T(8,128)} fusion(f32[1024,256]{1,0:T(8,128)} %all-reduce.8.cloned.1.call-done, f32[1024,1376]{0,1:T(8,128)} %param.3), kind=kOutput, calls=%fused_computation.3 | convolution fusion | flops 4328521728 | bytes 8093696 | tf_op jit(solution)/shard_map/dot_general | solution.py:16
  140.5 0.0 copy-start.2
  140.5 0.0 all-reduce.10.cloned.1.call-update
  140.5 0.2 all-reduce.12.cloned.1.call-start
  140.8 0.4 copy-done.2
  141.2 0.8 fusion.2
  142.0 95.4 %all-reduce.10.cloned.1.call-done = f32[1376,256]{1,0:T(8,128)} async-done(((f32[1376,256]{1,0:T(8,128)}), f32[1376,256]{1,0:T(8,128)}) %all-reduce.10.cloned.1.call-update) | async-done | bytes 1409040 | tf_op jit(solution)/shard_map/psum | solution.py:49
  237.4 0.0 copy-start.1
  237.4 3.1 broadcast_in_dim.2
  240.5 0.0 copy-done.1
  240.5 0.2 bitcast_multiply_fusion.2
  240.7 8.3 %convolution_bitcast_fusion.4 = f32[1024,256]{0,1:T(8,128)} fusion(f32[1376,256]{1,0:T(8,128)S(1)} %bitcast_multiply_fusion.2, f32[1024,1376]{0,1:T(8,128)} %param.3), kind=kOutput, calls=%fused_computation.20 | convolution fusion | flops 4328521728 | bytes 8093696 | tf_op jit(solution)/shard_map/dot_general | solution.py:12
  249.0 0.0 all-reduce.12.cloned.1.call-update
  249.0 0.0 all-reduce.14.cloned.1.call-start
  249.0 112.1 %all-reduce.12.cloned.1.call-done = f32[1024,256]{0,1:T(8,128)} async-done(((f32[1024,256]{0,1:T(8,128)}), f32[1024,256]{0,1:T(8,128)}) %all-reduce.12.cloned.1.call-update) | async-done | bytes 1048592 | tf_op jit(solution)/shard_map/psum | solution.py:46
  361.2 8.7 %convolution_bitcast_fusion.1 = f32[1376,256]{1,0:T(8,128)} fusion(f32[1024,256]{0,1:T(8,128)} %all-reduce.12.cloned.1.call-done, f32[1024,1376]{0,1:T(8,128)} %param.3), kind=kOutput, calls=%fused_computation.2 | convolution fusion | flops 4328521728 | bytes 8093696 | tf_op jit(solution)/shard_map/dot_general | solution.py:16
  369.9 0.0 all-reduce.14.cloned.1.call-update
  369.9 0.0 all-reduce.16.cloned.1.call-start
  369.9 4.7 multiply_reduce_fusion
  374.6 78.6 %psum.82 = f32[]{:T(128)} all-reduce(f32[]{:T(128)} %multiply_reduce_fusion), channel_id=1, replica_groups=mesh['tok'=16,'feat'=16] {'tok','feat'}, use_global_device_ids=true, to_apply=%region_7.8 | all-reduce | flops 1 | bytes 8 | tf_op jit(solution)/shard_map/psum | solution.py:42
  453.9 13.1 %all-reduce.14.cloned.1.call-done = f32[1376,256]{1,0:T(8,128)} async-done(((f32[1376,256]{1,0:T(8,128)}), f32[1376,256]{1,0:T(8,128)}) %all-reduce.14.cloned.1.call-update) | async-done | bytes 1409040 | tf_op jit(solution)/shard_map/psum | solution.py:49
  466.9 1.7 multiply_reduce_fusion.3
  468.6 25.5 %all-reduce = (f32[256]{0:T(256)S(1)}, f32[256]{0:T(256)S(1)}) all-reduce(f32[256]{0:T(256)S(1)} %get-tuple-element.3, f32[256]{0:T(256)S(1)} %get-tuple-element.2), channel_id=1, replica_groups=mesh['tok'=16,'feat'=16] {'feat'}, use_global_device_ids=true, to_apply=%region_3.4 | all-reduce | flops 512 | bytes 4096 | tf_op jit(solution)/shard_map/psum | solution.py:26
  494.1 2.8 multiply_reduce_fusion.2
  496.9 24.6 %psum.84 = f32[256]{0:T(256)S(1)} all-reduce(f32[256]{0:T(256)S(1)} %get-tuple-element.6), channel_id=1, replica_groups=mesh['tok'=16,'feat'=16] {'feat'}, use_global_device_ids=true, to_apply=%region_11.12 | all-reduce | flops 256 | bytes 2048 | tf_op jit(solution)/shard_map/psum | solution.py:26
  521.5 8.7 %convolution_bitcast_fusion.3 = f32[1024,256]{0,1:T(8,128)} fusion(f32[1024,1376]{0,1:T(8,128)} %param.3, f32[1376,256]{1,0:T(8,128)} %get-tuple-element.7, f32[1376,256]{1,0:T(8,128)S(1)} %bitcast_multiply_fusion.2, f32[256]{0:T(256)S(1)} %div.30), kind=kOutput, calls=%fused_computation.19 | convolution fusion | flops 4329226240 | bytes 9503744 | tf_op jit(solution)/shard_map/dot_general | solution.py:12
  530.1 0.0 all-reduce.16.cloned.1.call-update
  530.2 0.0 all-reduce.18.cloned.1.call-start
  530.2 109.2 %all-reduce.16.cloned.1.call-done = f32[1024,256]{0,1:T(8,128)} async-done(((f32[1024,256]{0,1:T(8,128)}), f32[1024,256]{0,1:T(8,128)}) %all-reduce.16.cloned.1.call-update) | async-done | bytes 1048592 | tf_op jit(solution)/shard_map/psum | solution.py:46
  639.4 8.7 %convolution_bitcast_fusion = f32[1376,256]{1,0:T(8,128)} fusion(f32[1024,256]{0,1:T(8,128)} %all-reduce.16.cloned.1.call-done, f32[1024,1376]{0,1:T(8,128)} %param.3), kind=kOutput, calls=%fused_computation.1 | convolution fusion | flops 4328521728 | bytes 8093696 | tf_op jit(solution)/shard_map/dot_general | solution.py:16
  648.1 0.0 all-reduce.18.cloned.1.call-update
  648.1 96.8 %all-reduce.18.cloned.1.call-done = f32[1376,256]{1,0:T(8,128)} async-done(((f32[1376,256]{1,0:T(8,128)}), f32[1376,256]{1,0:T(8,128)}) %all-reduce.18.cloned.1.call-update) | async-done | bytes 1409040 | tf_op jit(solution)/shard_map/psum | solution.py:49
  745.0 2.1 multiply_reduce_fusion.1
  747.1 25.3 %psum.87 = f32[256]{0:T(256)S(1)} all-reduce(f32[256]{0:T(256)S(1)} %multiply_reduce_fusion.1), channel_id=1, replica_groups=mesh['tok'=16,'feat'=16] {'feat'}, use_global_device_ids=true, to_apply=%region_15.16 | all-reduce | flops 256 | bytes 2048 | tf_op jit(solution)/shard_map/psum | solution.py:60
  772.4 3.8 multiply_subtract_fusion
  (4 shorter events, 0.0 us)
Async XLA Ops:
  7.2 1.1 copy-start
  7.2 124.7 %all-reduce.8.cloned.1.call-start = ((), (), s32[]{:S(2)}) async-start(), calls=%async_computation | async-start | bytes 2097152 | tf_op jit(solution)/shard_map/psum | solution.py:46
  16.5 220.9 %all-reduce.10.cloned.1.call-start = ((), (), s32[]{:S(2)}) async-start(), calls=%async_computation.1 | async-start | bytes 2818048 | tf_op jit(solution)/shard_map/psum | solution.py:49
  140.5 0.7 copy-start.2
  140.5 220.6 %all-reduce.12.cloned.1.call-start = ((), (), s32[]{:S(2)}) async-start(), calls=%async_computation.2 | async-start | bytes 2097152 | tf_op jit(solution)/shard_map/psum | solution.py:46
  237.4 3.1 copy-start.1
  249.0 217.9 %all-reduce.14.cloned.1.call-start = ((), (), s32[]{:S(2)}) async-start(), calls=%async_computation.3 | async-start | bytes 2818048 | tf_op jit(solution)/shard_map/psum | solution.py:49
  369.9 269.5 %all-reduce.16.cloned.1.call-start = ((), (), s32[]{:S(2)}) async-start(), calls=%async_computation.4 | async-start | bytes 2097152 | tf_op jit(solution)/shard_map/psum | solution.py:46
  530.2 214.8 %all-reduce.18.cloned.1.call-start = ((), (), s32[]{:S(2)}) async-start(), calls=%async_computation.5 | async-start | bytes 2818048 | tf_op jit(solution)/shard_map/psum | solution.py:49
Sparse Core Ops, SparseCore 0:
  16.6 115.1 all-reduce.7
  140.7 96.6 all-reduce.9
  249.1 112.0 all-reduce.11
  370.0 96.8 all-reduce.13
  530.3 109.0 all-reduce.15
  648.2 96.6 all-reduce.17
where the time goes:
time: 784 us; the launch traced here: 783 us
  waiting for transfers between devices  542 us (69%)
  blocking collectives  154 us (20%)
  matrix products  52 us (7%)
  other arithmetic  15.3 us (2%)
  between operations  14.8 us (2%)
    psum x3, waiting for transfers between devices, gram(): rows_out = lax.psum(matmul(calib, vec), 'feat')  337 us
    psum x3, waiting for transfers between devices, gram(): summed = lax.psum(partial_back, 'tok')  205 us
    psum x1, blocking collectives, on_device(): total = lax.psum(jnp.sum(calib * calib), ('tok', 'feat'))  78.6 us
    psum x2, blocking collectives, col_norm(): return lax.psum(jnp.sum(values * values, axis=0), 'feat')  50.1 us
    dot_general x3, matrix products, back_product(): lax.dot_general(left, right, (((0,), (0,)), ((), ())), precision=lax.Prec...  26 us
    dot_general x4, matrix products, matmul(): jnp.dot(left, right, precision=lax.Precision.HIGHEST, preferred_element_t...  25.9 us
    psum x1, blocking collectives, on_device(): curvature = lax.psum(jnp.sum(direction * image, axis=0), 'feat')  25.3 us
  transfers between devices with their start and end apart: 6, of which 6 were waited for; matrix products, arithmetic and copies ran while one was open for 1% of the time, Pallas kernels for 0%

commit v1 on v0

--- a/solution.py
+++ b/solution.py
@@ -46,7 +46,10 @@
         rows_out = lax.psum(matmul(calib, vec), "feat")
         partial_back = back_product(calib, rows_out)
         own_rows = lax.dynamic_slice_in_dim(rows_out, feat_place * share, share, 0)
-        summed = lax.psum(partial_back, "tok")
+        size, summed = (lax.axis_size("tok"), partial_back)
+        for reach in [1 << k for k in range(size.bit_length() - 1)]:
+            swap = [(i, i ^ reach) for i in range(size)]
+            summed = summed + lax.ppermute(summed, "tok", swap)
         return (live * summed, own_rows)
 
     targets, unused_rows = gram(teacher_w.astype(jnp.float32))

time: 784 us -> 950 us (1.21)
  waiting for transfers between devices: 542 us -> 662 us
  blocking collectives: 154 us -> 179 us
  starting transfers between devices: 0.43 us -> 25 us
    ppermute x0 -> x12, waiting for transfers between devices: none -> 322 us  [gram(): summed = summed + lax.ppermute(summed, 'tok', swap)]
    psum x3 -> x0, waiting for transfers between devices: 205 us -> none  [gram(): summed = lax.psum(partial_back, 'tok')]
    ppermute x0 -> x12, starting transfers between devices: none -> 24.9 us  [gram(): summed = summed + lax.ppermute(summed, 'tok', swap)]
    psum x1, blocking collectives: 78.6 us -> 101 us  [on_device(): total = lax.psum(jnp.sum(calib * calib), ('tok', 'feat'))]
  transfers between devices with their start and end apart: 6 -> 15, of which waited for: 6 -> 14; matrix products, arithmetic and copies ran while one was open for 1% -> 0% of each run, Pallas kernels for 0% -> 0%
where the time goes in v1:
time: 950 us; the launch traced here: 949 us
  waiting for transfers between devices  662 us (70%)
  blocking collectives  179 us (19%)
  matrix products  45.6 us (5%)
  starting transfers between devices  25 us (3%)
  other arithmetic  17.2 us (2%)
  between operations  14.6 us (2%)
    psum x3, waiting for transfers between devices, gram(): rows_out = lax.psum(matmul(calib, vec), 'feat')  340 us
    ppermute x12, waiting for transfers between devices, gram(): summed = summed + lax.ppermute(summed, 'tok', swap)  322 us
    psum x1, blocking collectives, on_device(): total = lax.psum(jnp.sum(calib * calib), ('tok', 'feat'))  101 us
    psum x2, blocking collectives, col_norm(): return lax.psum(jnp.sum(values * values, axis=0), 'feat')  49 us
    psum x1, blocking collectives, on_device(): curvature = lax.psum(jnp.sum(direction * image, axis=0), 'feat')  29.2 us
    ppermute x12, starting transfers between devices, gram(): summed = summed + lax.ppermute(summed, 'tok', swap)  24.9 us
    dot_general x4, matrix products, matmul(): jnp.dot(left, right, precision=lax.Precision.HIGHEST, preferred_element_t...  24.9 us
    dot_general x3, matrix products, back_product(): lax.dot_general(left, right, (((0,), (0,)), ((), ())), precision=lax.Prec...  20.7 us
  transfers between devices with their start and end apart: 15, of which 14 were waited for; matrix products, arithmetic and copies ran while one was open for 0% of the time, Pallas kernels for 0%

profile of v1, /device:TPU:1, one launch (start us, length us, event | category | flops | bytes accessed | tf_op | source)
XLA Modules:
  0.0 949.0 jit_solution(10649312876611879514)
XLA Ops:
  7.2 0.0 copy-start
  7.2 0.0 all-reduce.5.cloned.1.call-start
  7.2 1.0 copy-done
  8.3 8.2 fusion.9
  16.5 0.0 all-reduce.5.cloned.1.call-update
  16.5 0.0 all-reduce.7.cloned.1.call-start
  16.6 115.3 %all-reduce.5.cloned.1.call-done = f32[1024,256]{1,0:T(8,128)} async-done(((f32[1024,256]{1,0:T(8,128)}), f32[1024,256]{1,0:T(8,128)}) %all-reduce.5.cloned.1.call-update) | async-done | bytes 1048592 | tf_op jit(solution)/shard_map/psum | solution.py:46
  131.8 6.9 convolution_bitcast_fusion.2
  138.7 1.3 collective-permute-start
  140.0 30.4 %collective-permute-done = f32[1376,256]{1,0:T(8,128)S(1)} collective-permute-done((f32[1376,256]{1,0:T(8,128)S(1)}, f32[1376,256]{1,0:T(8,128)S(1)}, u32[]{:S(2)}, u32[]{:S(2)}) %collective-permute-start) | collective-permute-done | bytes 1409056 | tf_op jit(solution)/shard_map/ppermute | solution.py:52
  170.4 0.2 add.81
  170.6 2.8 collective-permute-start.1
  173.4 29.4 %collective-permute-done.1 = f32[1376,256]{1,0:T(8,128)S(1)} collective-permute-done((f32[1376,256]{1,0:T(8,128)S(1)}, f32[1376,256]{1,0:T(8,128)S(1)}, u32[]{:S(2)}, u32[]{:S(2)}) %collective-permute-start.1) | collective-permute-done | bytes 1409056 | tf_op jit(solution)/shard_map/ppermute | solution.py:52
  202.8 0.2 add.82
  203.0 1.3 collective-permute-start.2
  204.3 28.5 %collective-permute-done.2 = f32[1376,256]{1,0:T(8,128)S(1)} collective-permute-done((f32[1376,256]{1,0:T(8,128)S(1)}, f32[1376,256]{1,0:T(8,128)S(1)}, u32[]{:S(2)}, u32[]{:S(2)}) %collective-permute-start.2) | collective-permute-done | bytes 1409056 | tf_op jit(solution)/shard_map/ppermute | solution.py:52
  232.8 0.2 add.83
  233.0 3.0 collective-permute-start.3
  236.0 1.5 fusion.2
  237.5 0.0 slice-start.1
  237.5 27.5 %collective-permute-done.3 = f32[1376,256]{1,0:T(8,128)} collective-permute-done((f32[1376,256]{1,0:T(8,128)S(1)}, f32[1376,256]{1,0:T(8,128)}, u32[]{:S(2)}, u32[]{:S(2)}) %collective-permute-start.3) | collective-permute-done | bytes 1409056 | tf_op jit(solution)/shard_map/ppermute | solution.py:52
  265.0 3.1 broadcast_in_dim.2
  268.2 2.6 bitcast_multiply_fusion.2
  270.9 6.4 convolution_bitcast_fusion.4
  277.2 0.0 all-reduce.7.cloned.1.call-update
  277.2 0.0 all-reduce.9.cloned.1.call-start
  277.3 117.2 %all-reduce.7.cloned.1.call-done = f32[1024,256]{0,1:T(8,128)} async-done(((f32[1024,256]{0,1:T(8,128)}), f32[1024,256]{0,1:T(8,128)}) %all-reduce.7.cloned.1.call-update) | async-done | bytes 1048592 | tf_op jit(solution)/shard_map/psum | solution.py:46
  394.5 6.9 convolution_bitcast_fusion.1
  401.4 1.3 collective-permute-start.4
  402.7 30.4 %collective-permute-done.4 = f32[1376,256]{1,0:T(8,128)S(1)} collective-permute-done((f32[1376,256]{1,0:T(8,128)S(1)}, f32[1376,256]{1,0:T(8,128)S(1)}, u32[]{:S(2)}, u32[]{:S(2)}) %collective-permute-start.4) | collective-permute-done | bytes 1409056 | tf_op jit(solution)/shard_map/ppermute | solution.py:52
  433.1 0.2 add.85
  433.2 0.0 slice-start.3
  433.2 2.8 collective-permute-start.5
  436.0 29.4 %collective-permute-done.5 = f32[1376,256]{1,0:T(8,128)S(1)} collective-permute-done((f32[1376,256]{1,0:T(8,128)S(1)}, f32[1376,256]{1,0:T(8,128)S(1)}, u32[]{:S(2)}, u32[]{:S(2)}) %collective-permute-start.5) | collective-permute-done | bytes 1409056 | tf_op jit(solution)/shard_map/ppermute | solution.py:52
  465.5 0.2 add.86
  465.7 1.5 collective-permute-start.6
  467.2 28.5 %collective-permute-done.6 = f32[1376,256]{1,0:T(8,128)S(1)} collective-permute-done((f32[1376,256]{1,0:T(8,128)S(1)}, f32[1376,256]{1,0:T(8,128)S(1)}, u32[]{:S(2)}, u32[]{:S(2)}) %collective-permute-start.6) | collective-permute-done | bytes 1409056 | tf_op jit(solution)/shard_map/ppermute | solution.py:52
  495.7 1.3 add.87
  497.0 2.7 collective-permute-start.7
  499.7 2.1 multiply_reduce_fusion
  501.7 101.2 %psum.59 = f32[]{:T(128)} all-reduce(f32[]{:T(128)} %multiply_reduce_fusion), channel_id=1, replica_groups=mesh['tok'=16,'feat'=16] {'tok','feat'}, use_global_device_ids=true, to_apply=%region_5.6 | all-reduce | flops 1 | bytes 8 | tf_op jit(solution)/shard_map/psum | solution.py:42
  603.6 3.2 multiply_reduce_fusion.3
  606.8 23.5 %all-reduce = (f32[256]{0:T(256)S(1)}, f32[256]{0:T(256)S(1)}) all-reduce(f32[256]{0:T(256)S(1)} %get-tuple-element.3, f32[256]{0:T(256)S(1)} %get-tuple-element.2), channel_id=1, replica_groups=mesh['tok'=16,'feat'=16] {'feat'}, use_global_device_ids=true, to_apply=%region_2.3 | all-reduce | flops 512 | bytes 4096 | tf_op jit(solution)/shard_map/psum | solution.py:26
  630.4 1.6 multiply_reduce_fusion.2
  632.0 25.5 %psum.61 = f32[256]{0:T(256)S(1)} all-reduce(f32[256]{0:T(256)S(1)} %multiply_reduce_fusion.2), channel_id=1, replica_groups=mesh['tok'=16,'feat'=16] {'feat'}, use_global_device_ids=true, to_apply=%region_9.10 | all-reduce | flops 256 | bytes 2048 | tf_op jit(solution)/shard_map/psum | solution.py:26
  657.5 8.8 convolution_bitcast_fusion.3
  666.3 0.0 all-reduce.9.cloned.1.call-update
  666.3 107.6 %all-reduce.9.cloned.1.call-done = f32[1024,256]{0,1:T(8,128)} async-done(((f32[1024,256]{0,1:T(8,128)}), f32[1024,256]{0,1:T(8,128)}) %all-reduce.9.cloned.1.call-update) | async-done | bytes 1048592 | tf_op jit(solution)/shard_map/psum | solution.py:46
  773.9 6.9 convolution_bitcast_fusion
  780.8 1.3 collective-permute-start.8
  782.1 30.4 %collective-permute-done.8 = f32[1376,256]{1,0:T(8,128)S(1)} collective-permute-done((f32[1376,256]{1,0:T(8,128)S(1)}, f32[1376,256]{1,0:T(8,128)S(1)}, u32[]{:S(2)}, u32[]{:S(2)}) %collective-permute-start.8) | collective-permute-done | bytes 1409056 | tf_op jit(solution)/shard_map/ppermute | solution.py:52
  812.5 0.2 add.91
  812.7 2.8 collective-permute-start.9
  815.4 29.4 %collective-permute-done.9 = f32[1376,256]{1,0:T(8,128)S(1)} collective-permute-done((f32[1376,256]{1,0:T(8,128)S(1)}, f32[1376,256]{1,0:T(8,128)S(1)}, u32[]{:S(2)}, u32[]{:S(2)}) %collective-permute-start.9) | collective-permute-done | bytes 1409056 | tf_op jit(solution)/shard_map/ppermute | solution.py:52
  844.9 0.2 add.92
  845.1 1.3 collective-permute-start.10
  846.4 28.5 %collective-permute-done.10 = f32[1376,256]{1,0:T(8,128)S(1)} collective-permute-done((f32[1376,256]{1,0:T(8,128)S(1)}, f32[1376,256]{1,0:T(8,128)S(1)}, u32[]{:S(2)}, u32[]{:S(2)}) %collective-permute-start.10) | collective-permute-done | bytes 1409056 | tf_op jit(solution)/shard_map/ppermute | solution.py:52
  874.9 0.2 add.93
  875.1 2.9 collective-permute-start.11
  877.9 29.3 %collective-permute-done.11 = f32[1376,256]{1,0:T(8,128)S(1)} collective-permute-done((f32[1376,256]{1,0:T(8,128)S(1)}, f32[1376,256]{1,0:T(8,128)S(1)}, u32[]{:S(2)}, u32[]{:S(2)}) %collective-permute-start.11) | collective-permute-done | bytes 1409056 | tf_op jit(solution)/shard_map/ppermute | solution.py:52
  907.2 1.1 copy-done.6
  908.4 0.6 multiply_reduce_fusion.1
  908.9 29.2 %psum.63 = f32[256]{0:T(256)S(1)} all-reduce(f32[256]{0:T(256)S(1)} %multiply_reduce_fusion.1), channel_id=1, replica_groups=mesh['tok'=16,'feat'=16] {'feat'}, use_global_device_ids=true, to_apply=%region_12.13 | all-reduce | flops 256 | bytes 2048 | tf_op jit(solution)/shard_map/psum | solution.py:63
  938.1 4.4 multiply_subtract_fusion
  (24 shorter events, 0.1 us)
Async XLA Ops:
  7.2 1.1 copy-start
  7.2 124.7 %all-reduce.5.cloned.1.call-start = ((), (), s32[]{:S(2)}) async-start(), calls=%async_computation | async-start | bytes 2097152 | tf_op jit(solution)/shard_map/psum | solution.py:46
  16.5 378.0 %all-reduce.7.cloned.1.call-start = ((), (), s32[]{:S(2)}) async-start(), calls=%async_computation.1 | async-start | bytes 2097152 | tf_op jit(solution)/shard_map/psum | solution.py:46
  138.7 31.7 %collective-permute-start = (f32[1376,256]{1,0:T(8,128)S(1)}, f32[1376,256]{1,0:T(8,128)S(1)}, u32[]{:S(2)}, u32[]{:S(2)}) collective-permute-start(f32[1376,256]{1,0:T(8,128)S(1)} %convolution_bitcast_fusion.2), channel_id=1, source_target_pairs={{0,16},{16,0},{32,48},{48,32},{64,80},{80,64},{96,112},{112,96},{1... | collective-permute-start | bytes 4227080 | tf_op jit(solution)/shard_map/ppermute | solution.py:52
  170.6 32.2 %collective-permute-start.1 = (f32[1376,256]{1,0:T(8,128)S(1)}, f32[1376,256]{1,0:T(8,128)S(1)}, u32[]{:S(2)}, u32[]{:S(2)}) collective-permute-start(f32[1376,256]{1,0:T(8,128)S(1)} %add.81), channel_id=1, source_target_pairs={{0,32},{16,48},{32,0},{48,16},{64,96},{80,112},{96,64},{112,80},{1... | collective-permute-start | bytes 4227080 | tf_op jit(solution)/shard_map/ppermute | solution.py:52
  203.0 29.8 %collective-permute-start.2 = (f32[1376,256]{1,0:T(8,128)S(1)}, f32[1376,256]{1,0:T(8,128)S(1)}, u32[]{:S(2)}, u32[]{:S(2)}) collective-permute-start(f32[1376,256]{1,0:T(8,128)S(1)} %add.82), channel_id=1, source_target_pairs={{0,64},{16,80},{32,96},{48,112},{64,0},{80,16},{96,32},{112,48},{1... | collective-permute-start | bytes 4227080 | tf_op jit(solution)/shard_map/ppermute | solution.py:52
  232.8 38.0 %slice-start = ((s8[5636096]{0:T(1024)(128)(4,1)}), s8[1441792]{0:T(1024)(128)(4,1)S(1)}, s32[]{:S(2)}) async-start(s8[5636096]{0:T(1024)(128)(4,1)} %bitcast.35), calls=%async_computation.3 | async-start | bytes 2883584
  233.0 35.2 %copy-start.5 = (f32[1376,256]{1,0:T(8,128)}, f32[1376,256]{1,0:T(8,128)S(1)}, u32[]{:S(2)}) copy-start(f32[1376,256]{1,0:T(8,128)S(1)} %add.83) | copy-start | bytes 4227076
  233.0 32.0 %collective-permute-start.3 = (f32[1376,256]{1,0:T(8,128)S(1)}, f32[1376,256]{1,0:T(8,128)}, u32[]{:S(2)}, u32[]{:S(2)}) collective-permute-start(f32[1376,256]{1,0:T(8,128)S(1)} %add.83), channel_id=1, source_target_pairs={{0,128},{16,144},{32,160},{48,176},{64,192},{80,208},{96,224},{112... | collective-permute-start | bytes 4227080 | tf_op jit(solution)/shard_map/ppermute | solution.py:52
  237.5 33.3 %slice-start.1 = ((s8[5636096]{0:T(1024)(128)(4,1)}), s8[4194304]{0:T(1024)(128)(4,1)S(1)}, s32[]{:S(2)}) async-start(s8[5636096]{0:T(1024)(128)(4,1)} %bitcast.35), calls=%async_computation.4 | async-start | bytes 8388608
  268.2 2.7 copy-start.1
  277.2 496.7 %all-reduce.9.cloned.1.call-start = ((), (), s32[]{:S(2)}) async-start(), calls=%async_computation.2 | async-start | bytes 2097152 | tf_op jit(solution)/shard_map/psum | solution.py:46
  401.4 31.6 %collective-permute-start.4 = (f32[1376,256]{1,0:T(8,128)S(1)}, f32[1376,256]{1,0:T(8,128)S(1)}, u32[]{:S(2)}, u32[]{:S(2)}) collective-permute-start(f32[1376,256]{1,0:T(8,128)S(1)} %convolution_bitcast_fusion.1), channel_id=1, source_target_pairs={{0,16},{16,0},{32,48},{48,32},{64,80},{80,64},{96,112},{112,96},{1... | collective-permute-start | bytes 4227080 | tf_op jit(solution)/shard_map/ppermute | solution.py:52
  433.1 66.6 %slice-start.2 = ((s8[5636096]{0:T(1024)(128)(4,1)}), s8[4194304]{0:T(1024)(128)(4,1)S(1)}, s32[]{:S(2)}) async-start(s8[5636096]{0:T(1024)(128)(4,1)} %bitcast.37), calls=%async_computation.5 | async-start | bytes 8388608
  433.2 66.4 %slice-start.3 = ((s8[5636096]{0:T(1024)(128)(4,1)}), s8[1441792]{0:T(1024)(128)(4,1)S(1)}, s32[]{:S(2)}) async-start(s8[5636096]{0:T(1024)(128)(4,1)} %bitcast.37), calls=%async_computation.6 | async-start | bytes 2883584
  433.2 32.2 %collective-permute-start.5 = (f32[1376,256]{1,0:T(8,128)S(1)}, f32[1376,256]{1,0:T(8,128)S(1)}, u32[]{:S(2)}, u32[]{:S(2)}) collective-permute-start(f32[1376,256]{1,0:T(8,128)S(1)} %add.85), channel_id=1, source_target_pairs={{0,32},{16,48},{32,0},{48,16},{64,96},{80,112},{96,64},{112,80},{1... | collective-permute-start | bytes 4227080 | tf_op jit(solution)/shard_map/ppermute | solution.py:52
  465.7 30.0 %collective-permute-start.6 = (f32[1376,256]{1,0:T(8,128)S(1)}, f32[1376,256]{1,0:T(8,128)S(1)}, u32[]{:S(2)}, u32[]{:S(2)}) collective-permute-start(f32[1376,256]{1,0:T(8,128)S(1)} %add.86), channel_id=1, source_target_pairs={{0,64},{16,80},{32,96},{48,112},{64,0},{80,16},{96,32},{112,48},{1... | collective-permute-start | bytes 4227080 | tf_op jit(solution)/shard_map/ppermute | solution.py:52
  497.0 106.6 %copy-start.2 = (f32[1376,2,128]{2,1,0:T(2,128)S(1)}, f32[1376,2,128]{2,1,0:T(2,128)}, u32[]{:S(2)}) copy-start(f32[1376,2,128]{2,1,0:T(2,128)} %copy-done.1) | copy-start | bytes 4227076
  497.0 106.6 %collective-permute-start.7 = (f32[1376,256]{1,0:T(8,128)}, f32[1376,256]{1,0:T(8,128)}, u32[]{:S(2)}, u32[]{:S(2)}) collective-permute-start(f32[1376,256]{1,0:T(8,128)} %add.87), channel_id=1, source_target_pairs={{0,128},{16,144},{32,160},{48,176},{64,192},{80,208},{96,224},{112... | collective-permute-start | bytes 4227080 | tf_op jit(solution)/shard_map/ppermute | solution.py:52
  780.8 31.6 %collective-permute-start.8 = (f32[1376,256]{1,0:T(8,128)S(1)}, f32[1376,256]{1,0:T(8,128)S(1)}, u32[]{:S(2)}, u32[]{:S(2)}) collective-permute-start(f32[1376,256]{1,0:T(8,128)S(1)} %convolution_bitcast_fusion), channel_id=1, source_target_pairs={{0,16},{16,0},{32,48},{48,32},{64,80},{80,64},{96,112},{112,96},{1... | collective-permute-start | bytes 4227080 | tf_op jit(solution)/shard_map/ppermute | solution.py:52
  812.7 32.2 %collective-permute-start.9 = (f32[1376,256]{1,0:T(8,128)S(1)}, f32[1376,256]{1,0:T(8,128)S(1)}, u32[]{:S(2)}, u32[]{:S(2)}) collective-permute-start(f32[1376,256]{1,0:T(8,128)S(1)} %add.91), channel_id=1, source_target_pairs={{0,32},{16,48},{32,0},{48,16},{64,96},{80,112},{96,64},{112,80},{1... | collective-permute-start | bytes 4227080 | tf_op jit(solution)/shard_map/ppermute | solution.py:52
  845.1 63.3 %copy-start.3 = (f32[1376,256]{1,0:T(8,128)S(1)}, f32[1376,256]{1,0:T(8,128)}, u32[]{:S(2)}) copy-start(f32[1376,256]{1,0:T(8,128)} %get-tuple-element.6) | copy-start | bytes 4227076
  845.1 29.8 %collective-permute-start.10 = (f32[1376,256]{1,0:T(8,128)S(1)}, f32[1376,256]{1,0:T(8,128)S(1)}, u32[]{:S(2)}, u32[]{:S(2)}) collective-permute-start(f32[1376,256]{1,0:T(8,128)S(1)} %add.92), channel_id=1, source_target_pairs={{0,64},{16,80},{32,96},{48,112},{64,0},{80,16},{96,32},{112,48},{1... | collective-permute-start | bytes 4227080 | tf_op jit(solution)/shard_map/ppermute | solution.py:52
  875.1 32.2 %copy-start.4 = (f32[1376,256]{1,0:T(8,128)}, f32[1376,256]{1,0:T(8,128)S(1)}, u32[]{:S(2)}) copy-start(f32[1376,256]{1,0:T(8,128)S(1)} %add.93) | copy-start | bytes 4227076
  875.1 32.2 %collective-permute-start.11 = (f32[1376,256]{1,0:T(8,128)S(1)}, f32[1376,256]{1,0:T(8,128)S(1)}, u32[]{:S(2)}, u32[]{:S(2)}) collective-permute-start(f32[1376,256]{1,0:T(8,128)S(1)} %add.93), channel_id=1, source_target_pairs={{0,128},{16,144},{32,160},{48,176},{64,192},{80,208},{96,224},{112... | collective-permute-start | bytes 4227080 | tf_op jit(solution)/shard_map/ppermute | solution.py:52
  907.2 1.1 copy-start.6
Sparse Core Ops, SparseCore 0:
  16.6 115.1 all-reduce.4
  277.4 117.0 all-reduce.6
  666.4 107.4 all-reduce.8
